TPU v7x, 32 devices: a whole 2x2x4 slice. The times are simulated.
32 devices in a mesh: dp: 4 (over x, core), expert: 8 (over z, y).
Axes of the slice: x: 2, y: 2, z: 4, core: 2. Of those that a mesh axis runs over, the one named last changes fastest.
Arguments:
- hidden: bfloat16 [2048, 8, 1536], P(('dp', 'expert')), may hold values from -6 to 6
- routes: int32 [2048, 8], P(('dp', 'expert')), may hold values from 0 to 15, all different within a row; in each aligned block of 64 rows (0 to 63, 64 to 127, ...) at most 48 rows name the same one
- gate_scores: int32 [2048, 8], P(('dp', 'expert')), may hold values from 1 to 64
- down_weight: bfloat16 [16, 1536, 4096], P('expert', None, 'dp'), may hold values from -0.15625 to 0.15625
Outputs:
- output: bfloat16 [2048, 4096], P(('dp', 'expert'))
- gram: float32 [16, 1536, 1536], P('expert', 'dp')
Inputs may be any that keep to these rules, and one draw needn't show every extreme that they name: `routes`: each token names 8 different experts. Among the 64 tokens of one device no expert is named more than 48 times, and on some devices one expert is named exactly 48 times. Every expert is named by some token.
All inputs are finite; a program needn't handle non-finite values.
Results may differ from a plain program's by a relative error of at most 0.005.
Values may be sent and summed in bfloat16 or wider, within the bound.
A program may use at most 128 MiB of HBM per device.

v0:
```python
import jax
import jax.numpy as jnp
from jax import lax
from jax.sharding import PartitionSpec as P


def local(hidden, routes, gate_scores, down_weight):
    tokens = hidden.shape[0]
    top_count = hidden.shape[1]
    hidden_width = hidden.shape[2]
    n_owner = lax.axis_size("expert")
    n_group = lax.axis_size("dp")
    per_owner = down_weight.shape[0]
    experts = n_owner * per_owner
    pair_total = tokens * top_count
    capacity = 3 * tokens * top_count // (2 * experts)
    flat_routes = routes.reshape(pair_total)
    onehot = (flat_routes[:, None] == jnp.arange(experts, dtype=jnp.int32)[None, :]).astype(
        jnp.int32
    )
    before = jnp.cumsum(onehot, axis=0) - onehot
    position = jnp.sum(before * onehot, axis=1)
    slot_index = flat_routes * capacity + position
    local_counts = jnp.sum(onehot, axis=0).astype(jnp.float32)
    totals = lax.psum(local_counts, ("dp", "expert"))
    pair_rows = hidden.reshape(pair_total, hidden_width)
    outgoing = (
        jnp.zeros((experts * capacity, hidden_width), jnp.bfloat16).at[slot_index].set(pair_rows)
    )
    outgoing = outgoing.reshape(n_owner, per_owner, capacity, hidden_width)
    arrived = lax.all_to_all(outgoing, "expert", split_axis=0, concat_axis=0, tiled=True)
    everyone = lax.all_gather(arrived, "dp", axis=0, tiled=True)
    own_counts = lax.dynamic_slice_in_dim(
        totals, lax.axis_index("expert") * per_owner, per_owner, 0
    )
    block_width = hidden_width // n_group
    my_columns = lax.dynamic_slice_in_dim(
        everyone, lax.axis_index("dp") * block_width, block_width, 3
    )
    gram_rows = jnp.einsum(
        "sxcf,sxcg->xfg", my_columns, everyone, preferred_element_type=jnp.float32
    )
    results = jnp.einsum(
        "sxcf,xfd->sxcd", everyone, down_weight, preferred_element_type=jnp.float32
    ).astype(jnp.bfloat16)
    returned = lax.all_to_all(
        lax.all_to_all(results, "dp", split_axis=0, concat_axis=3, tiled=True),
        "expert",
        split_axis=0,
        concat_axis=0,
        tiled=True,
    )
    gram = gram_rows / own_counts[:, None, None]
    model_width = returned.shape[3]
    pair_results = returned.reshape(experts * capacity, model_width)[slot_index]
    scores = gate_scores.astype(jnp.float32)
    weight = scores / jnp.sum(scores, axis=1, keepdims=True)
    combined = jnp.sum(
        pair_results.reshape(tokens, top_count, model_width).astype(jnp.float32)
        * weight[:, :, None],
        axis=1,
    )
    return (combined.astype(jnp.bfloat16), gram)


def solution(mesh):
    placed = (
        P(("dp", "expert"), None, None),
        P(("dp", "expert"), None),
        P(("dp", "expert"), None),
        P("expert", None, "dp"),
    )
    return jax.shard_map(
        local,
        mesh=mesh,
        in_specs=placed,
        out_specs=(P(("dp", "expert"), None), P("expert", "dp", None)),
        check_vma=False,
    )
```

profile of v0, /device:TPU:0, one launch (start us, length us, event | category | flops | bytes accessed | tf_op | source)
XLA Modules:
  0.0 453.1 jit_solution(3097682405529023763)
XLA Ops:
  7.2 0.0 copy-start
  7.2 0.0 all-gather.2.cloned.1.call-start
  7.2 0.9 copy.15
  8.1 0.1 eq.29
  8.2 0.1 eq.25
  8.3 0.7 broadcast_multiply_fusion
  9.0 1.1 reduce-window.6
  10.1 0.2 slice_reduce_fusion
  10.4 0.1 copy.14
  10.5 0.1 mul.35
  10.6 0.1 convert_reduce_fusion
  10.7 0.0 copy-done
  10.7 4.7 %scatter_custom_fusion = bf16[768,1536]{1,0:T(8,128)(2,1)} fusion(s32[512]{0:T(512)S(1)} %bitcast.42, bf16[64,8,1536]{2,1,0:T(8,128)(2,1)S(1)} %copy-done, bf16[]{:T(256)} %constant.11.clone.1), kind=kCustom, calls=%fused_computation.10 | custom fusion | bytes 3932162 | tf_op jit(solution)/shard_map/scatter | solution.py:28
  15.4 61.2 %all_to_all.28 = bf16[8,2,48,1536]{3,2,1,0:T(8,128)(2,1)S(1)} all-to-all(bf16[8,2,48,1536]{3,2,1,0:T(8,128)(2,1)} %bitcast.41), channel_id=1, replica_groups=mesh['dp'=4,'expert'=8] {'expert'}, dimensions={0} | all-to-all | bytes 4718592 | tf_op jit(solution)/shard_map/all_to_all | solution.py:31
  76.6 1.6 copy.18
  78.1 0.0 all-gather.2.cloned.1.call-update
  78.2 63.4 %all-gather.2.cloned.1.call-done = bf16[32,2,48,1536]{3,2,0,1:T(8,128)(2,1)} async-done(((bf16[8,2,48,1536]{3,2,0,1:T(8,128)(2,1)}), bf16[32,2,48,1536]{3,2,0,1:T(8,128)(2,1)}) %all-gather.2.cloned.1.call-update) | async-done | bytes 9437200 | tf_op jit(solution)/shard_map/all_gather | solution.py:32
  141.5 14.3 %convert_bitcast_fusion = bf16[32,2,48,1024]{3,2,0,1:T(8,128)(2,1)S(1)} fusion(bf16[32,2,48,1536]{3,2,0,1:T(8,128)(2,1)} %all-gather.2.cloned.1.call-done, bf16[2,1536,1024]{2,1,0:T(8,128)(2,1)} %param.7), kind=kOutput, calls=%fused_computation.7 | convolution fusion | flops 9666822144 | bytes 22020096 | tf_op jit(solution)/shard_map/sxcf,xfd->sxcd/dot_general | solution.py:43
  155.9 1.3 copy.19
  157.2 74.2 %all_to_all.29 = bf16[32,2,48,1024]{3,2,1,0:T(8,128)(2,1)} all-to-all(bf16[32,2,48,1024]{3,2,1,0:T(8,128)(2,1)S(1)} %copy.19), channel_id=1, replica_groups=mesh['dp'=4,'expert'=8] {'dp'}, dimensions={0} | all-to-all | bytes 12582912 | tf_op jit(solution)/shard_map/all_to_all | solution.py:47
  231.4 10.8 %copy.27 = bf16[4,8,2,48,1024]{4,0,3,2,1:T(4,128)(2,1)} copy(bf16[4,8,2,48,1024]{4,3,2,1,0:T(8,128)(2,1)} %bitcast.39) | data formatting | bytes 12582912 | tf_op jit(solution)/shard_map/all_to_all | solution.py:47
  242.2 11.1 %all_to_all.23 = bf16[8,2,48,4096]{3,2,1,0:T(8,128)(2,1)} reshape(bf16[8,2,48,4,1024]{4,3,2,1,0:T(4,128)(2,1)} %bitcast.40) | data formatting | bytes 12582912 | tf_op jit(solution)/shard_map/all_to_all | solution.py:47
  253.2 0.0 copy-start.2
  253.2 5.6 %all-to-all-start.2 = ((bf16[8,2,48,4096]{3,2,1,0:T(8,128)(2,1)}), bf16[8,2,48,4096]{3,2,1,0:T(8,128)(2,1)}, u32[]{:S(2)}, u32[]{:S(2)}) async-start(bf16[8,2,48,4096]{3,2,1,0:T(8,128)(2,1)} %all_to_all.23), calls=%async_computation.2 | async-start | bytes 12582912 | tf_op jit(solution)/shard_map/all_to_all | solution.py:46
  258.9 157.9 %psum.7 = f32[16]{0:T(128)S(1)} all-reduce(f32[16]{0:T(128)S(1)} %convert_element_type.36), channel_id=1, replica_groups=mesh['dp'=4,'expert'=8] {'dp','expert'}, use_global_device_ids=true, to_apply=%region_7.8 | all-reduce | flops 16 | bytes 128 | tf_op jit(solution)/shard_map/psum | solution.py:25
  416.8 0.0 copy-done.2
  416.8 0.1 copy.21
  416.9 0.1 dynamic_slice.7
  417.0 10.5 %bitcast_divide_fusion = f32[2,384,1536]{2,1,0:T(8,128)} fusion(bf16[32,2,48,1536]{3,2,0,1:T(8,128)(2,1)} %all-gather.2.cloned.1.call-done, f32[2]{0:T(128)S(1)} %dynamic_slice.7, s32[]{:T(128)S(6)} %select_n.18), kind=kOutput, calls=%fused_computation.8 | convolution fusion | flops 3625058304 | bytes 16515084 | tf_op jit(solution)/shard_map/sxcf,sxcg->xfg/dot_general | solution.py:40
  427.5 0.0 all-to-all-done.2
  427.5 0.0 copy-start.1
  427.5 12.3 %gather_fusion = bf16[512,4096]{1,0:T(8,128)(2,1)} fusion(bf16[768,4096]{1,0:T(8,128)(2,1)} %bitcast.10, s32[1024]{0:T(1024)S(1)} %pad_clamp_fusion), kind=kCustom, calls=%fused_computation | custom fusion | bytes 8390656 | tf_op jit(solution)/shard_map/gather | solution.py:55
  439.8 6.5 %fusion = bf16[64,4096]{1,0:T(8,128)(2,1)} fusion(bf16[512,4096]{1,0:T(8,128)(2,1)} %gather_fusion, f32[64,8]{1,0:T(8,128)S(1)} %copy.21), kind=kLoop, calls=%fused_computation.3 | loop fusion | flops 6029312 | bytes 4720640 | tf_op jit(solution)/shard_map/reduce_sum | solution.py:58
  446.2 0.0 copy-done.1
  (8 shorter events, 0.1 us)
Async XLA Ops:
  7.2 3.6 copy-start
  7.2 134.4 %all-gather.2.cloned.1.call-start = ((), (), s32[]{:S(2)}) async-start(), calls=%async_computation.3 | async-start | bytes 11796480 | tf_op jit(solution)/shard_map/all_gather | solution.py:32
  253.2 163.6 %copy-start.2 = (s32[64,8]{0,1:T(8,128)S(1)}, s32[64,8]{0,1:T(8,128)}, u32[]{:S(2)}) copy-start(s32[64,8]{0,1:T(8,128)} %param.6) | copy-start | bytes 6148
  253.2 174.3 %all-to-all-start.2 = ((bf16[8,2,48,4096]{3,2,1,0:T(8,128)(2,1)}), bf16[8,2,48,4096]{3,2,1,0:T(8,128)(2,1)}, u32[]{:S(2)}, u32[]{:S(2)}) async-start(bf16[8,2,48,4096]{3,2,1,0:T(8,128)(2,1)} %all_to_all.23), calls=%async_computation.2 | async-start | bytes 12582912 | tf_op jit(solution)/shard_map/all_to_all | solution.py:46
  427.5 18.7 %copy-start.1 = (bf16[64,8,1536]{2,1,0:T(8,128)(2,1)S(1)}, bf16[64,8,1536]{2,1,0:T(8,128)(2,1)}, u32[]{:S(2)}) copy-start(bf16[64,8,1536]{2,1,0:T(8,128)(2,1)} %param.4) | copy-start | bytes 4718596
Sparse Core Ops, SparseCore 0:
  78.3 63.2 all-gather.1
where the time goes:
time: 454 us; the launch traced here: 453 us
  blocking collectives  293 us (65%)
  waiting for transfers between devices  63.4 us (14%)
  local copies, waits for them, and re-layouts  43.3 us (10%)
  matrix products  24.8 us (5%)
  between operations  14.1 us (3%)
  other arithmetic  8.53 us (2%)
  starting transfers between devices  5.69 us (1%)
    psum x1, blocking collectives, local(): totals = lax.psum(local_counts, ('dp', 'expert'))  158 us
    all_to_all x1, blocking collectives, local(): lax.all_to_all(results, 'dp', split_axis=0, concat_axis=3, tiled=True)  74.2 us
    all_gather x1, waiting for transfers between devices, local(): everyone = lax.all_gather(arrived, 'dp', axis=0, tiled=True)  63.4 us
    all_to_all x1, blocking collectives, local(): lax.all_to_all(outgoing, 'expert', split_axis=0, concat_axis=0, tiled=True)  61.2 us
    all_to_all x2, local copies, waits for them, and re-layouts, local(): lax.all_to_all(results, 'dp', split_axis=0, concat_axis=3, tiled=True)  21.9 us
    dot_general x1, matrix products, local(): jnp.einsum('sxcf,xfd->sxcd', everyone, down_weight, preferred_element_typ...  14.3 us
    gather x1, local copies, waits for them, and re-layouts, local(): pair_results = returned.reshape(experts * capacity, model_width)[slot_index]  12.3 us
    dot_general x1, matrix products, local(): jnp.einsum('sxcf,sxcg->xfg', my_columns, everyone, preferred_element_type...  10.5 us
  transfers between devices with their start and end apart: 2, of which 1 were waited for; matrix products, arithmetic and copies ran while one was open for 2% of the time, Pallas kernels for 0%

commit v1 on v0

--- a/solution.py
+++ b/solution.py
@@ -1,7 +1,42 @@
+import functools
 import jax
 import jax.numpy as jnp
 from jax import lax
 from jax.sharding import PartitionSpec as P
+
+
+def end_cycles(field, array_dim, inp):
+    v1 = field.shape
+    w2 = field.reshape(*v1[:array_dim], inp, v1[array_dim] // inp, *v1[array_dim + 1 :])
+    return jnp.moveaxis(w2, array_dim, 0)
+
+
+def change_shelves_on_mesh(x_in, in_dim):
+    x_in = jnp.moveaxis(x_in, 0, in_dim)
+    a_next = x_in.shape
+    return x_in.reshape(
+        *a_next[:in_dim], a_next[in_dim] * a_next[in_dim + 1], *a_next[in_dim + 2 :]
+    )
+
+
+def follow_pages(tile_in, lane_axis, sample, panel):
+    tall = lax.axis_index(lane_axis)
+    long_array = lax.axis_size(lane_axis)
+    carry_out, earlier = (long_array, tall)
+    block_last = end_cycles(tile_in, sample, carry_out)
+    cards = [block_last[earlier]]
+    for dev in range(1, carry_out):
+        o_now = block_last[(earlier + dev) % carry_out]
+        cards.append(
+            lax.ppermute(
+                o_now, lane_axis, [(idx, (idx + dev) % carry_out) for idx in range(carry_out)]
+            )
+        )
+    block_last = jnp.stack(cards)[(earlier - jnp.arange(carry_out)) % carry_out]
+    return change_shelves_on_mesh(block_last, panel)
+
+
+edge_meet = functools.partial(follow_pages, lane_axis="expert", sample=0, panel=0)
 
 
 def local(hidden, routes, gate_scores, down_weight):
@@ -28,7 +63,7 @@
         jnp.zeros((experts * capacity, hidden_width), jnp.bfloat16).at[slot_index].set(pair_rows)
     )
     outgoing = outgoing.reshape(n_owner, per_owner, capacity, hidden_width)
-    arrived = lax.all_to_all(outgoing, "expert", split_axis=0, concat_axis=0, tiled=True)
+    arrived = edge_meet(outgoing)
     everyone = lax.all_gather(arrived, "dp", axis=0, tiled=True)
     own_counts = lax.dynamic_slice_in_dim(
         totals, lax.axis_index("expert") * per_owner, per_owner, 0

time: 454 us -> 468 us (1.031)
  blocking collectives: 293 us -> 232 us
  waiting for transfers between devices: 63.4 us -> 109 us
  starting transfers between devices: 5.69 us -> 22.5 us
  local copies, waits for them, and re-layouts: 43.3 us -> 56.3 us
    all_to_all x1 -> x0, blocking collectives: 61.2 us -> none  [local(): lax.all_to_all(outgoing, 'expert', split_axis=0, concat_axis=0, tiled=True)]
    ppermute x0 -> x7, waiting for transfers between devices: none -> 38.7 us  [follow_pages(): lax.ppermute(o_now, lane_axis, [(idx, (idx + dev) % carry_out) for idx in...]
    ppermute x0 -> x7, starting transfers between devices: none -> 16.8 us  [follow_pages(): lax.ppermute(o_now, lane_axis, [(idx, (idx + dev) % carry_out) for idx in...]
    gather x0 -> x2, local copies, waits for them, and re-layouts: none -> 7 us  [follow_pages(): block_last = jnp.stack(cards)[(earlier - jnp.arange(carry_out)) % carry_out]]
    all_gather x1, waiting for transfers between devices: 63.4 us -> 70.2 us  [local(): everyone = lax.all_gather(arrived, 'dp', axis=0, tiled=True)]
  transfers between devices with their start and end apart: 2 -> 9, of which waited for: 1 -> 5; matrix products, arithmetic and copies ran while one was open for 2% -> 3% of each run, Pallas kernels for 0% -> 0%
where the time goes in v1:
time: 468 us
  blocking collectives  232 us (50%)
  waiting for transfers between devices  109 us (23%)
  local copies, waits for them, and re-layouts  56.3 us (12%)
  matrix products  24.8 us (5%)
  starting transfers between devices  22.5 us (5%)
  between operations  14.2 us (3%)
  other arithmetic  8.64 us (2%)
    psum x1, blocking collectives, local(): totals = lax.psum(local_counts, ('dp', 'expert'))  158 us
    all_to_all x1, blocking collectives, local(): lax.all_to_all(results, 'dp', split_axis=0, concat_axis=3, tiled=True)  74.2 us
    all_gather x1, waiting for transfers between devices, local(): everyone = lax.all_gather(arrived, 'dp', axis=0, tiled=True)  70.2 us
    ppermute x7, waiting for transfers between devices, follow_pages(): lax.ppermute(o_now, lane_axis, [(idx, (idx + dev) % carry_out) for idx in...  38.7 us
    all_to_all x2, local copies, waits for them, and re-layouts, local(): lax.all_to_all(results, 'dp', split_axis=0, concat_axis=3, tiled=True)  21.9 us
    ppermute x7, starting transfers between devices, follow_pages(): lax.ppermute(o_now, lane_axis, [(idx, (idx + dev) % carry_out) for idx in...  16.8 us
    dot_general x1, matrix products, local(): jnp.einsum('sxcf,xfd->sxcd', everyone, down_weight, preferred_element_typ...  14.3 us
    gather x1, local copies, waits for them, and re-layouts, local(): pair_results = returned.reshape(experts * capacity, model_width)[slot_index]  12.3 us
  transfers between devices with their start and end apart: 9, of which 5 were waited for; matrix products, arithmetic and copies ran while one was open for 3% of the time, Pallas kernels for 0%

profile of v1, /device:TPU:0, one launch (start us, length us, event | category | flops | bytes accessed | tf_op | source)
XLA Modules:
  0.0 467.6 jit_solution(17987717781669559724)
XLA Ops:
  7.2 0.0 copy-start
  7.2 0.0 all-gather.3.cloned.1.call-start
  7.3 0.8 broadcast_multiply_fusion
  8.1 0.8 copy.15
  8.9 0.1 eq.39
  9.0 0.1 eq.35
  9.1 0.1 copy.14
  9.1 0.1 mul.35
  9.3 1.2 reduce-window.6
  10.4 0.2 slice_reduce_fusion
  10.7 0.1 convert_reduce_fusion
  10.9 4.7 scatter_custom_fusion
  15.5 2.5 dynamic-slice_bitcast_fusion
  18.0 3.0 collective-permute-start
  21.0 3.0 collective-permute-start.6
  24.1 2.0 collective-permute-start.5
  26.1 0.0 collective-permute-start.4
  26.1 3.0 collective-permute-start.3
  29.1 4.6 collective-permute-done
  33.6 1.6 collective-permute-start.1
  35.2 0.7 bitcast_dynamic-update-slice_fusion.6
  35.9 22.0 %collective-permute-done.1 = bf16[1,2,48,1536]{3,2,1,0:T(8,128)(2,1)S(1)} collective-permute-done((bf16[1,2,48,1536]{3,2,1,0:T(8,128)(2,1)S(1)}, bf16[1,2,48,1536]{3,2,1,0:T(8,128)(2,1)S(1)}, u32[]{:S(2)}, u32[]{:S(2)}) %collective-permute-start.1) | collective-permute-done | bytes 294944 | tf_op jit(solution)/shard_map/ppermute | solution.py:31
  57.9 4.2 collective-permute-start.2
  62.2 0.7 bitcast_dynamic-update-slice_fusion.5
  62.9 6.7 %collective-permute-done.2 = bf16[1,2,48,1536]{3,2,1,0:T(8,128)(2,1)S(1)} collective-permute-done((bf16[1,2,48,1536]{3,2,1,0:T(8,128)(2,1)S(1)}, bf16[1,2,48,1536]{3,2,1,0:T(8,128)(2,1)S(1)}, u32[]{:S(2)}, u32[]{:S(2)}) %collective-permute-start.2) | collective-permute-done | bytes 294944 | tf_op jit(solution)/shard_map/ppermute | solution.py:31
  69.6 0.7 bitcast_dynamic-update-slice_fusion.4
  70.3 5.4 %collective-permute-done.3 = bf16[1,2,48,1536]{3,2,1,0:T(8,128)(2,1)S(1)} collective-permute-done((bf16[1,2,48,1536]{3,2,1,0:T(8,128)(2,1)S(1)}, bf16[1,2,48,1536]{3,2,1,0:T(8,128)(2,1)S(1)}, u32[]{:S(2)}, u32[]{:S(2)}) %collective-permute-start.3) | collective-permute-done | bytes 294944 | tf_op jit(solution)/shard_map/ppermute | solution.py:31
  75.8 0.7 bitcast_dynamic-update-slice_fusion.3
  76.5 0.0 collective-permute-done.4
  76.5 0.7 bitcast_dynamic-update-slice_fusion.2
  77.2 0.7 bitcast_dynamic-update-slice_fusion.1
  78.0 0.8 bitcast_dynamic-update-slice_fusion
  78.7 3.8 gather_fusion
  82.5 3.2 copy.18
  85.8 0.0 all-gather.3.cloned.1.call-update
  85.8 70.2 %all-gather.3.cloned.1.call-done = bf16[32,2,48,1536]{3,2,0,1:T(8,128)(2,1)} async-done(((bf16[8,2,48,1536]{3,2,0,1:T(8,128)(2,1)}), bf16[32,2,48,1536]{3,2,0,1:T(8,128)(2,1)}) %all-gather.3.cloned.1.call-update) | async-done | bytes 9437200 | tf_op jit(solution)/shard_map/all_gather | solution.py:67
  156.0 14.3 %convert_bitcast_fusion = bf16[32,2,48,1024]{3,2,0,1:T(8,128)(2,1)S(1)} fusion(bf16[32,2,48,1536]{3,2,0,1:T(8,128)(2,1)} %all-gather.3.cloned.1.call-done, bf16[2,1536,1024]{2,1,0:T(8,128)(2,1)} %param.7), kind=kOutput, calls=%fused_computation.8 | convolution fusion | flops 9666822144 | bytes 22020096 | tf_op jit(solution)/shard_map/sxcf,xfd->sxcd/dot_general | solution.py:78
  170.3 1.3 copy.19
  171.7 74.2 %all_to_all.23 = bf16[32,2,48,1024]{3,2,1,0:T(8,128)(2,1)} all-to-all(bf16[32,2,48,1024]{3,2,1,0:T(8,128)(2,1)S(1)} %copy.19), channel_id=1, replica_groups=mesh['dp'=4,'expert'=8] {'dp'}, dimensions={0} | all-to-all | bytes 12582912 | tf_op jit(solution)/shard_map/all_to_all | solution.py:82
  245.9 10.8 %copy.27 = bf16[4,8,2,48,1024]{4,0,3,2,1:T(4,128)(2,1)} copy(bf16[4,8,2,48,1024]{4,3,2,1,0:T(8,128)(2,1)} %bitcast.71) | data formatting | bytes 12582912 | tf_op jit(solution)/shard_map/all_to_all | solution.py:82
  256.7 11.1 %all_to_all.19 = bf16[8,2,48,4096]{3,2,1,0:T(8,128)(2,1)} reshape(bf16[8,2,48,4,1024]{4,3,2,1,0:T(4,128)(2,1)} %bitcast.72) | data formatting | bytes 12582912 | tf_op jit(solution)/shard_map/all_to_all | solution.py:82
  267.7 5.6 %all-to-all-start.1 = ((bf16[8,2,48,4096]{3,2,1,0:T(8,128)(2,1)}), bf16[8,2,48,4096]{3,2,1,0:T(8,128)(2,1)}, u32[]{:S(2)}, u32[]{:S(2)}) async-start(bf16[8,2,48,4096]{3,2,1,0:T(8,128)(2,1)} %all_to_all.19), calls=%async_computation.1 | async-start | bytes 12582912 | tf_op jit(solution)/shard_map/all_to_all | solution.py:81
  273.4 157.9 %psum.7 = f32[16]{0:T(128)S(1)} all-reduce(f32[16]{0:T(128)S(1)} %convert_element_type.36), channel_id=1, replica_groups=mesh['dp'=4,'expert'=8] {'dp','expert'}, use_global_device_ids=true, to_apply=%region_7.8 | all-reduce | flops 16 | bytes 128 | tf_op jit(solution)/shard_map/psum | solution.py:60
  431.3 0.1 copy.21
  431.4 0.1 dynamic_slice.39
  431.5 10.5 %bitcast_divide_fusion = f32[2,384,1536]{2,1,0:T(8,128)} fusion(bf16[32,2,48,1536]{3,2,0,1:T(8,128)(2,1)} %all-gather.3.cloned.1.call-done, f32[2]{0:T(128)S(1)} %dynamic_slice.39, s32[]{:T(128)S(6)} %select_n.113), kind=kOutput, calls=%fused_computation.9 | convolution fusion | flops 3625058304 | bytes 16515084 | tf_op jit(solution)/shard_map/sxcf,sxcg->xfg/dot_general | solution.py:75
  442.0 12.3 %gather_fusion.1 = bf16[512,4096]{1,0:T(8,128)(2,1)} fusion(bf16[768,4096]{1,0:T(8,128)(2,1)} %bitcast.26, s32[1024]{0:T(1024)S(1)} %pad_clamp_fusion), kind=kCustom, calls=%fused_computation.1 | custom fusion | bytes 8390656 | tf_op jit(solution)/shard_map/gather | solution.py:90
  454.3 6.5 %fusion = bf16[64,4096]{1,0:T(8,128)(2,1)} fusion(bf16[512,4096]{1,0:T(8,128)(2,1)} %gather_fusion.1, f32[64,8]{1,0:T(8,128)S(1)} %copy.21), kind=kLoop, calls=%fused_computation.4 | loop fusion | flops 6029312 | bytes 4720640 | tf_op jit(solution)/shard_map/reduce_sum | solution.py:93
  (18 shorter events, 0.1 us)
Async XLA Ops:
  7.2 3.7 copy-start
  7.2 148.8 %all-gather.3.cloned.1.call-start = ((), (), s32[]{:S(2)}) async-start(), calls=%async_computation.2 | async-start | bytes 11796480 | tf_op jit(solution)/shard_map/all_gather | solution.py:67
  18.0 15.6 %collective-permute-start = (bf16[1,2,48,1536]{3,2,1,0:T(8,128)(2,1)S(1)}, bf16[1,2,48,1536]{3,2,1,0:T(8,128)(2,1)S(1)}, u32[]{:S(2)}, u32[]{:S(2)}) collective-permute-start(bf16[1,2,48,1536]{3,2,1,0:T(8,128)(2,1)S(1)} %get-tuple-element.10), channel_id=1, source_target_pairs={{0,1},{1,2},{2,3},{3,4},{4,5},{5,6},{6,7},{7,0},{8,9},{9,10},{10,1... | collective-permute-start | bytes 884744 | tf_op jit(solution)/shard_map/ppermute | solution.py:31
  21.0 56.9 %collective-permute-start.6 = (bf16[1,2,48,1536]{3,2,1,0:T(8,128)(2,1)S(1)}, bf16[1,2,48,1536]{3,2,1,0:T(8,128)(2,1)S(1)}, u32[]{:S(2)}, u32[]{:S(2)}) collective-permute-start(bf16[1,2,48,1536]{3,2,1,0:T(8,128)(2,1)S(1)} %get-tuple-element.4), channel_id=1, source_target_pairs={{0,7},{1,0},{2,1},{3,2},{4,3},{5,4},{6,5},{7,6},{8,15},{9,8},{10,9... | collective-permute-start | bytes 884744 | tf_op jit(solution)/shard_map/ppermute | solution.py:31
  24.1 53.2 %collective-permute-start.5 = (bf16[1,2,48,1536]{3,2,1,0:T(8,128)(2,1)S(1)}, bf16[1,2,48,1536]{3,2,1,0:T(8,128)(2,1)S(1)}, u32[]{:S(2)}, u32[]{:S(2)}) collective-permute-start(bf16[1,2,48,1536]{3,2,1,0:T(8,128)(2,1)S(1)} %get-tuple-element.5), channel_id=1, source_target_pairs={{0,6},{1,7},{2,0},{3,1},{4,2},{5,3},{6,4},{7,5},{8,14},{9,15},{10,... | collective-permute-start | bytes 884744 | tf_op jit(solution)/shard_map/ppermute | solution.py:31
  26.1 50.5 %collective-permute-start.4 = (bf16[1,2,48,1536]{3,2,1,0:T(8,128)(2,1)S(1)}, bf16[1,2,48,1536]{3,2,1,0:T(8,128)(2,1)S(1)}, u32[]{:S(2)}, u32[]{:S(2)}) collective-permute-start(bf16[1,2,48,1536]{3,2,1,0:T(8,128)(2,1)S(1)} %get-tuple-element.6), channel_id=1, source_target_pairs={{0,5},{1,6},{2,7},{3,0},{4,1},{5,2},{6,3},{7,4},{8,13},{9,14},{10,... | collective-permute-start | bytes 884744 | tf_op jit(solution)/shard_map/ppermute | solution.py:31
  26.1 49.7 %collective-permute-start.3 = (bf16[1,2,48,1536]{3,2,1,0:T(8,128)(2,1)S(1)}, bf16[1,2,48,1536]{3,2,1,0:T(8,128)(2,1)S(1)}, u32[]{:S(2)}, u32[]{:S(2)}) collective-permute-start(bf16[1,2,48,1536]{3,2,1,0:T(8,128)(2,1)S(1)} %get-tuple-element.7), channel_id=1, source_target_pairs={{0,4},{1,5},{2,6},{3,7},{4,0},{5,1},{6,2},{7,3},{8,12},{9,13},{10,... | collective-permute-start | bytes 884744 | tf_op jit(solution)/shard_map/ppermute | solution.py:31
  33.6 24.3 %collective-permute-start.1 = (bf16[1,2,48,1536]{3,2,1,0:T(8,128)(2,1)S(1)}, bf16[1,2,48,1536]{3,2,1,0:T(8,128)(2,1)S(1)}, u32[]{:S(2)}, u32[]{:S(2)}) collective-permute-start(bf16[1,2,48,1536]{3,2,1,0:T(8,128)(2,1)S(1)} %get-tuple-element.9), channel_id=1, source_target_pairs={{0,2},{1,3},{2,4},{3,5},{4,6},{5,7},{6,0},{7,1},{8,10},{9,11},{10,... | collective-permute-start | bytes 884744 | tf_op jit(solution)/shard_map/ppermute | solution.py:31
  57.9 11.7 %collective-permute-start.2 = (bf16[1,2,48,1536]{3,2,1,0:T(8,128)(2,1)S(1)}, bf16[1,2,48,1536]{3,2,1,0:T(8,128)(2,1)S(1)}, u32[]{:S(2)}, u32[]{:S(2)}) collective-permute-start(bf16[1,2,48,1536]{3,2,1,0:T(8,128)(2,1)S(1)} %get-tuple-element.8), channel_id=1, source_target_pairs={{0,3},{1,4},{2,5},{3,6},{4,7},{5,0},{6,1},{7,2},{8,11},{9,12},{10,... | collective-permute-start | bytes 884744 | tf_op jit(solution)/shard_map/ppermute | solution.py:31
  267.7 163.6 %copy-start.2 = (s32[64,8]{0,1:T(8,128)S(1)}, s32[64,8]{0,1:T(8,128)}, u32[]{:S(2)}) copy-start(s32[64,8]{0,1:T(8,128)} %param.6) | copy-start | bytes 6148
  267.7 174.3 %all-to-all-start.1 = ((bf16[8,2,48,4096]{3,2,1,0:T(8,128)(2,1)}), bf16[8,2,48,4096]{3,2,1,0:T(8,128)(2,1)}, u32[]{:S(2)}, u32[]{:S(2)}) async-start(bf16[8,2,48,4096]{3,2,1,0:T(8,128)(2,1)} %all_to_all.19), calls=%async_computation.1 | async-start | bytes 12582912 | tf_op jit(solution)/shard_map/all_to_all | solution.py:81
  442.0 18.7 %copy-start.1 = (bf16[64,8,1536]{2,1,0:T(8,128)(2,1)S(1)}, bf16[64,8,1536]{2,1,0:T(8,128)(2,1)}, u32[]{:S(2)}) copy-start(bf16[64,8,1536]{2,1,0:T(8,128)(2,1)} %param.4) | copy-start | bytes 4718596
Sparse Core Ops, SparseCore 0:
  85.9 70.0 all-gather.2
